TPU v7x, 32 devices: a whole 2x2x4 slice. The times are simulated.
32 devices in a mesh: seq: 16 (over z, x, core), head: 2 (over y).
Axes of the slice: x: 2, y: 2, z: 4, core: 2. Of those that a mesh axis runs over, the one named last changes fastest.
Arguments:
- features: bfloat16 [8, 32, 8, 512], P(None, 'seq', 'head'), may hold values from -540 to 540
- gn_gain: float32 [512], replicated, may hold values from 0.5 to 1.5
- gn_bias: float32 [512], replicated, may hold values from -3 to 3
- conv_weight: bfloat16 [3, 3, 3, 16, 512], replicated, may hold values from -0.0546875 to 0.0546875
- conv_bias: float32 [16], replicated, may hold values from -3 to 3
- patch_weight: bfloat16 [64, 3072], replicated, may hold values from -0.75 to 0.75
- patch_bias: float32 [3072], replicated, may hold values from -3 to 3
- image_mod: float32 [3, 3072], replicated, may hold values from -3 to 3
- w_qkv: bfloat16 [3072, 3, 2048], P('seq', None, 'head'), may hold values from -5 to 5
- text_ids: int32 [512], replicated, may hold values from 0 to 16383
- text_length: int32 [1], replicated, may hold values from 256 to 512
- text_table: bfloat16 [3072, 16384], P('seq'), may hold values from -60 to 60
- text_mod: float32 [2, 3072], P(None, 'seq'), may hold values from -3 to 3
- w_text: bfloat16 [3072, 2, 2048], P('seq', None, 'head'), may hold values from -2 to 2
- w_out: bfloat16 [2048, 3072], P('head'), may hold values from -0.625 to 0.625
- out_bias: float32 [3072], replicated, may hold values from -3 to 3
Outputs:
- block_out: bfloat16 [8, 16, 4, 3072], P(None, 'seq', 'head')
All inputs are finite; a program needn't handle non-finite values.
Results may differ from a plain program's by a relative error of at most 0.0089.
Values may be sent and summed in bfloat16 or wider, within the bound.
A program may use at most 128 MiB of HBM per device.

v0:
```python
import math
import jax
import jax.numpy as jnp
from jax import lax
from jax.sharding import PartitionSpec as P

HD = 128
GN_GROUPS = 32
eps_norm = 1e-06


def with_halo(cells, sides, width):
    for axis, dim in sides:
        count = lax.axis_size(axis)
        ends = count - 1
        head = lax.slice_in_dim(cells, 0, width, axis=dim)
        tail = lax.slice_in_dim(cells, cells.shape[dim] - width, cells.shape[dim], axis=dim)
        cells = jnp.concatenate(
            [
                lax.ppermute(tail, axis, [(i, (i + 1) % count) for i in range(ends)]),
                cells,
                lax.ppermute(head, axis, [((i + 1) % count, i) for i in range(ends)]),
            ],
            axis=dim,
        )
    return cells


def patchify(latent):
    frame_count, row_count, col_count, chan_count = latent.shape
    blocks = latent.reshape(frame_count, row_count // 2, 2, col_count // 2, 2, chan_count)
    blocks = blocks.transpose(0, 1, 3, 2, 4, 5)
    return blocks.reshape(frame_count * (row_count // 2) * (col_count // 2), 4 * chan_count)


def embed_tokens(patches, patch_weight, patch_bias, image_mod):
    hidden = jnp.dot(patches, patch_weight, preferred_element_type=jnp.float32) + patch_bias
    center = jnp.mean(hidden, axis=1, keepdims=True)
    offset = hidden - center
    spread = jnp.mean(offset * offset, axis=1, keepdims=True)
    normed = offset * lax.rsqrt(spread + eps_norm)
    modulated = (normed * (1.0 + image_mod[1]) + image_mod[0]).astype(jnp.bfloat16)
    return (hidden, modulated)


def text_start(query, text_keys, text_values, text_valid):
    scores = jnp.einsum("qhe,khe->qhk", query, text_keys, preferred_element_type=jnp.float32) / HD
    scores = jnp.where(text_valid[None, None, :], scores, -1e30)
    first_top = jnp.max(scores, axis=2)
    probs = jnp.exp(scores - first_top[..., None])
    first_total = jnp.sum(probs, axis=2)
    first_acc = jnp.einsum(
        "qhk,khe->qhe", probs.astype(jnp.bfloat16), text_values, preferred_element_type=jnp.float32
    )
    return (first_top, first_total, first_acc)


def attend_rows(query, state, piece):
    piece_rows = piece.shape[0]
    block_rows = math.gcd(piece_rows, 2048)
    heads_count = query.shape[1]
    blocks = piece.reshape(piece_rows // block_rows, block_rows, 2, heads_count, HD)

    def one_block(inner, block):
        run_top, run_total, run_acc = inner
        scores = (
            jnp.einsum("qhe,khe->qhk", query, block[:, 0], preferred_element_type=jnp.float32) / HD
        )
        new_top = jnp.maximum(run_top, jnp.max(scores, axis=2))
        factor = jnp.exp(run_top - new_top)
        probs = jnp.exp(scores - new_top[..., None])
        run_total = run_total * factor + jnp.sum(probs, axis=2)
        run_acc = run_acc * factor[..., None] + jnp.einsum(
            "qhk,khe->qhe",
            probs.astype(jnp.bfloat16),
            block[:, 1],
            preferred_element_type=jnp.float32,
        )
        return ((new_top, run_total, run_acc), None)

    return lax.scan(one_block, state, blocks)[0]


def body(
    features,
    gn_gain,
    gn_bias,
    conv_weight,
    conv_bias,
    patch_weight,
    patch_bias,
    image_mod,
    w_qkv,
    text_ids,
    text_length,
    text_table,
    text_mod,
    w_text,
    w_out,
    out_bias,
):
    frame_count, row_count, col_count, chan_count = features.shape
    width_full = patch_weight.shape[1]
    values = features.astype(jnp.float32)
    grouped = values.reshape(frame_count, row_count, col_count, GN_GROUPS, chan_count // GN_GROUPS)
    group_sums = jnp.sum(grouped, axis=(0, 1, 2, 4))
    group_squares = jnp.sum(grouped * grouped, axis=(0, 1, 2, 4))
    group_sums, group_squares = lax.psum((group_sums, group_squares), ("seq", "head"))
    cell_count = (
        frame_count
        * row_count
        * col_count
        * (chan_count // GN_GROUPS)
        * lax.axis_size("seq")
        * lax.axis_size("head")
    )
    group_mean = group_sums / cell_count
    group_scale = lax.rsqrt(group_squares / cell_count - group_mean * group_mean + eps_norm)
    normed = ((grouped - group_mean[:, None]) * group_scale[:, None]).reshape(
        frame_count, row_count, col_count, chan_count
    )
    activated = jax.nn.silu(normed * gn_gain + gn_bias).astype(jnp.bfloat16)
    rimmed = with_halo(activated, (("seq", 1), ("head", 2)), 1)
    padded = jnp.concatenate([rimmed[:1], rimmed[:1], rimmed], axis=0)
    windows = []
    for time_off in range(3):
        for row_off in range(3):
            for col_off in range(3):
                windows.append(
                    padded[
                        time_off : time_off + frame_count,
                        row_off : row_off + row_count,
                        col_off : col_off + col_count,
                    ]
                )
    stacked = jnp.stack(windows, axis=3)
    latent_chans = conv_weight.shape[3]
    kernels = conv_weight.reshape(27, latent_chans, chan_count)
    latent_sum = jnp.einsum("fyxkc,kzc->fyxz", stacked, kernels, preferred_element_type=jnp.float32)
    latent = (latent_sum + conv_bias).astype(jnp.bfloat16)
    patches = patchify(latent)
    hidden, own_modulated = embed_tokens(patches, patch_weight, patch_bias, image_mod)
    modulated = lax.all_gather(own_modulated, "head", axis=0, tiled=True)
    token_count = modulated.shape[0]
    head_width = w_qkv.shape[2]
    heads_here = head_width // HD
    qkv = jnp.einsum(
        "nd,dkj->nkj",
        modulated,
        lax.all_gather(w_qkv, "seq", axis=0, tiled=True),
        preferred_element_type=jnp.float32,
    ).astype(jnp.bfloat16)
    context = jnp.take(text_table, text_ids, axis=1).astype(jnp.float32)
    text_weight = w_text.astype(jnp.float32)
    text_gain = 1.0 + text_mod[1]
    text_shift = text_mod[0]
    text_sums, text_squares = lax.psum(
        (jnp.sum(context, axis=0), jnp.sum(context * context, axis=0)), "seq"
    )
    text_mean = text_sums / width_full
    text_scale = lax.rsqrt(text_squares / width_full - text_mean * text_mean + eps_norm)
    text_normed = (context - text_mean) * text_scale * text_gain[:, None] + text_shift[:, None]
    partial_kv = jnp.einsum(
        "dt,dkj->tkj", text_normed, text_weight, precision=lax.Precision.HIGHEST
    )
    text_kv = lax.psum(partial_kv, "seq")
    text_kv = text_kv.astype(jnp.bfloat16)
    text_count = text_kv.shape[0]
    text_valid = jnp.arange(text_count, dtype=jnp.int32) < text_length[0]
    query = qkv[:, 0].reshape(token_count, heads_here, HD)
    text_keys = text_kv[:, 0].reshape(text_count, heads_here, HD)
    text_values = text_kv[:, 1].reshape(text_count, heads_here, HD)
    first_state = text_start(query, text_keys, text_values, text_valid)
    image_kv = qkv[:, 1:3]
    run_top, run_total, run_acc = attend_rows(
        query, first_state, lax.all_gather(image_kv, "seq", axis=0, tiled=True)
    )
    attended = (
        (run_acc / run_total[..., None]).astype(jnp.bfloat16).reshape(token_count, head_width)
    )
    projected = (
        lax.psum_scatter(
            jnp.dot(attended, w_out, preferred_element_type=jnp.float32),
            "head",
            scatter_dimension=0,
            tiled=True,
        )
        + out_bias
    )
    block_out = (hidden + image_mod[2] * projected).astype(jnp.bfloat16)
    return block_out.reshape(frame_count, row_count // 2, col_count // 2, width_full)


def solution(mesh):
    return jax.shard_map(
        body,
        mesh=mesh,
        in_specs=(
            P(None, "seq", "head", None),
            P(),
            P(),
            P(),
            P(),
            P(),
            P(),
            P(),
            P("seq", None, "head"),
            P(),
            P(),
            P("seq", None),
            P(None, "seq"),
            P("seq", None, "head"),
            P("head", None),
            P(),
        ),
        out_specs=P(None, "seq", "head", None),
        check_vma=False,
    )
```

profile of v0, /device:TPU:0, one launch (start us, length us, event | category | flops | bytes accessed | tf_op | source)
XLA Modules:
  0.0 285.2 jit_solution(11076966553390359524)
XLA Ops:
  6.5 0.7 all-gather.3.cloned.1.call-update
  7.3 0.9 convert_reduce_fusion.1
  8.6 43.1 %all-reduce = (f32[32]{0:T(128)S(1)}, f32[32]{0:T(128)S(1)}) all-reduce(f32[32]{0:T(128)S(1)} %reduce_sum.92, f32[32]{0:T(128)S(1)} %reduce_sum.89), channel_id=1, replica_groups=mesh['seq'=16,'head'=2] {'seq','head'}, use_global_device_ids=true, to_apply=%region_5.6 | all-reduce | flops 64 | bytes 512 | tf_op jit(solution)/shard_map/psum | solution.py:108
  52.0 1.0 fusion.41
  52.9 1.8 collective-permute-start
  54.7 1.3 collective-permute-start.1
  56.7 1.0 fusion.78
  57.7 0.7 compare_and_fusion
  58.4 1.5 collective-permute-done.1
  59.9 2.5 collective-permute-start.2
  62.4 1.3 collective-permute-start.3
  63.7 10.1 %copy.82 = bf16[192,16384]{0,1:T(8,128)(2,1)} copy(bf16[192,16384]{1,0:T(8,128)(2,1)} %param.27) | data formatting | bytes 12582912 | tf_op args[11]
  73.8 6.2 %gather_fusion = bf16[512,192]{1,0:T(8,128)(2,1)S(1)} fusion(bf16[192,16384]{0,1:T(8,128)(2,1)} %copy.82, s32[1024]{0:T(1024)S(1)} %pad_clamp_fusion), kind=kCustom, calls=%fused_computation | custom fusion | bytes 395264 | tf_op jit(solution)/shard_map/jit(_take)/gather | solution.py:153
  82.9 5.9 %all_gather.9 = bf16[32,3072]{1,0:T(8,128)(2,1)S(1)} all-gather(bf16[16,3072]{1,0:T(8,128)(2,1)S(1)} %add_convert_fusion.1), channel_id=1, replica_groups=mesh['seq'=16,'head'=2] {'head'}, dimensions={0}, use_global_device_ids=true | all-gather | bytes 294912 | tf_op jit(solution)/shard_map/all_gather | solution.py:143
  88.8 23.2 %all-gather.3.cloned.1.call-done = bf16[3072,3,1024]{2,0,1:T(8,128)(2,1)} async-done(((bf16[192,3,1024]{2,0,1:T(8,128)(2,1)}), bf16[3072,3,1024]{2,0,1:T(8,128)(2,1)}) %all-gather.3.cloned.1.call-update) | async-done | bytes 18874384 | tf_op jit(solution)/shard_map/all_gather | solution.py:150
  112.0 9.7 %convolution_convert_fusion = bf16[32,3,1024]{2,0,1:T(8,128)(2,1)S(1)} fusion(bf16[3072,3,1024]{2,0,1:T(8,128)(2,1)} %all-gather.3.cloned.1.call-done, bf16[32,3072]{1,0:T(8,128)(2,1)S(1)} %all_gather.9), kind=kOutput, calls=%fused_computation.7 | convolution fusion | flops 604078080 | bytes 19267584 | tf_op jit(solution)/shard_map/nd,dkj->nkj/dot_general | solution.py:147
  122.8 33.0 %all-reduce.1 = (f32[512]{0:T(512)S(1)}, f32[512]{0:T(512)S(1)}) all-reduce(f32[512]{0:T(512)S(1)} %get-tuple-element.16, f32[512]{0:T(512)S(1)} %get-tuple-element.15), channel_id=1, replica_groups=mesh['seq'=16,'head'=2] {'seq'}, use_global_device_ids=true, to_apply=%region_9.10 | all-reduce | flops 1024 | bytes 8192 | tf_op jit(solution)/shard_map/psum | solution.py:157
  155.8 3.9 %fusion.12 = f32[512,2,1024]{2,0,1:T(8,128)} fusion(bf16[192,2,1024]{2,1,0:T(2,128)(2,1)S(1)} %copy-done, f32[192]{0:T(256)S(1)} %bitcast.263, f32[192]{0:T(256)S(1)} %bitcast.262, f32[512]{0:T(512)S(1)} %get-tuple-element.47, f32[512]{0:T(512)S(1)} %get-tuple-element.46, bf16[512,192]{1,0:T(8,128)(2,1)S(1)} %gather_fusion, ...), kind=kOutput, calls=%fused_computation.24 | convolution fusion | flops 2416508928 | bytes 5183488 | tf_op jit(solution)/shard_map/dt,dkj->tkj/dot_general | solution.py:163
  159.7 94.6 %all-reduce.3 = bf16[512,2,1024]{2,0,1:T(8,128)(2,1)S(1)} all-reduce(f32[512,2,1024]{2,0,1:T(8,128)} %fusion.12), channel_id=1, replica_groups=mesh['seq'=16,'head'=2] {'seq'}, use_global_device_ids=true, to_apply=%region_10.11 | all-reduce | flops 1048576 | bytes 6291456 | tf_op jit(solution)/shard_map/psum | solution.py:166
  255.8 1.3 fusion.80
  257.0 2.4 copy.103
  261.9 1.9 fusion.43
  263.9 13.2 %reduce-scatter.2.cloned.1.call-done = f32[16,3072]{1,0:T(8,128)} async-done(((f32[32,3072]{1,0:T(8,128)}), f32[16,3072]{1,0:T(8,128)}) %reduce-scatter.2.cloned.1.call-update) | async-done | bytes 196624 | tf_op jit(solution)/shard_map/reduce_scatter | solution.py:182
  277.1 1.0 add_convert_fusion
  (106 shorter events, 9.0 us)
Async XLA Ops:
  6.5 149.3 %copy-start = (bf16[192,2,1024]{2,1,0:T(2,128)(2,1)S(1)}, bf16[192,2,1024]{2,1,0:T(2,128)(2,1)}, u32[]{:S(2)}) copy-start(bf16[192,2,1024]{2,1,0:T(2,128)(2,1)} %param.29) | copy-start | bytes 2359300
  6.5 105.4 %all-gather.3.cloned.1.call-start = ((), (), s32[]{:S(2)}) async-start(), calls=%async_computation.1 | async-start | bytes 20054016 | tf_op jit(solution)/shard_map/all_gather | solution.py:150
  7.3 249.8 %all-gather.5.cloned.1.call-start = ((), (), s32[]{:S(2)}) async-start(), calls=%async_computation.2 | async-start | bytes 2228224 | tf_op jit(solution)/shard_map/all_gather | solution.py:176
  52.9 5.4 %collective-permute-start = (bf16[8,1,4,512]{3,0,2,1:T(8,128)(2,1)S(1)}, bf16[8,1,4,512]{3,0,2,1:T(8,128)(2,1)S(1)}, u32[]{:S(2)}, u32[]{:S(2)}) collective-permute-start(bf16[8,1,4,512]{3,0,2,1:T(8,128)(2,1)S(1)} %get-tuple-element.41), channel_id=1, source_target_pairs={{0,2},{2,4},{4,6},{6,8},{8,10},{10,12},{12,14},{14,16},{16,18},{18... | collective-permute-start | bytes 98312 | tf_op jit(solution)/shard_map/ppermute | solution.py:20
  54.7 5.2 %collective-permute-start.1 = (bf16[8,1,4,512]{3,0,2,1:T(8,128)(2,1)S(1)}, bf16[8,1,4,512]{3,0,2,1:T(8,128)(2,1)S(1)}, u32[]{:S(2)}, u32[]{:S(2)}) collective-permute-start(bf16[8,1,4,512]{3,0,2,1:T(8,128)(2,1)S(1)} %get-tuple-element.42), channel_id=1, source_target_pairs={{2,0},{4,2},{6,4},{8,6},{10,8},{12,10},{14,12},{16,14},{18,16},{20... | collective-permute-start | bytes 98312 | tf_op jit(solution)/shard_map/ppermute | solution.py:22
  59.9 20.1 %collective-permute-start.2 = (bf16[8,4,1,512]{3,0,2,1:T(8,128)(2,1)S(1)}, bf16[8,4,1,512]{3,0,2,1:T(8,128)(2,1)S(1)}, u32[]{:S(2)}, u32[]{:S(2)}) collective-permute-start(bf16[8,4,1,512]{3,0,2,1:T(8,128)(2,1)S(1)} %get-tuple-element.39), channel_id=1, source_target_pairs={{0,1},{2,3},{4,5},{6,7},{8,9},{10,11},{12,13},{14,15},{16,17},{18,... | collective-permute-start | bytes 98312 | tf_op jit(solution)/shard_map/ppermute | solution.py:20
  62.4 17.6 %collective-permute-start.3 = (bf16[8,4,1,512]{3,0,2,1:T(8,128)(2,1)S(1)}, bf16[8,4,1,512]{3,0,2,1:T(8,128)(2,1)S(1)}, u32[]{:S(2)}, u32[]{:S(2)}) collective-permute-start(bf16[8,4,1,512]{3,0,2,1:T(8,128)(2,1)S(1)} %get-tuple-element.40), channel_id=1, source_target_pairs={{1,0},{3,2},{5,4},{7,6},{9,8},{11,10},{13,12},{15,14},{17,16},{19,... | collective-permute-start | bytes 98312 | tf_op jit(solution)/shard_map/ppermute | solution.py:22
  80.3 0.8 copy-start.1
  80.4 0.8 copy-start.7
  80.4 0.8 copy-start.8
  80.5 1.0 copy-start.3
  80.5 1.0 copy-start.9
  80.8 1.5 copy-start.4
  80.8 1.5 copy-start.5
  88.8 67.0 %copy-start.10 = (f32[2,192]{1,0:T(2,128)S(1)}, f32[2,192]{1,0:T(2,128)}, u32[]{:S(2)}) copy-start(f32[2,192]{1,0:T(2,128)} %param.28) | copy-start | bytes 4612
  122.4 154.7 %reduce-scatter.2.cloned.1.call-start = ((), (), s32[]{:S(2)}) async-start(), calls=%async_computation.3 | async-start | bytes 589824 | tf_op jit(solution)/shard_map/reduce_scatter | solution.py:182
  257.0 4.9 %slice-start = ((s8[6291456]{0:T(1024)(128)(4,1)}), s8[4194304]{0:T(1024)(128)(4,1)S(1)}, s32[]{:S(2)}) async-start(s8[6291456]{0:T(1024)(128)(4,1)} %bitcast.249), calls=%async_computation.4 | async-start | bytes 8388608
  259.4 2.5 slice-start.1
  259.6 1.2 copy-start.2
  261.9 15.2 %copy-start.6 = (f32[3072]{0:T(1024)S(1)}, f32[3072]{0:T(1024)}, u32[]{:S(2)}) copy-start(f32[3072]{0:T(1024)} %param.31) | copy-start | bytes 36868
Sparse Core Ops, SparseCore 0:
  8.9 103.0 all-gather.2
  122.5 42.3 all-gather.4
  264.0 12.9 reduce-scatter.1
where the time goes:
time: 286 us; the launch traced here: 285 us
  blocking collectives  177 us (62%)
  waiting for transfers between devices  38.6 us (13%)
  local copies, waits for them, and re-layouts  22.7 us (8%)
  matrix products  19.1 us (7%)
  between operations  14.3 us (5%)
  starting transfers between devices  6.94 us (2%)
  other arithmetic  6.94 us (2%)
    psum x1, blocking collectives, body(): text_kv = lax.psum(partial_kv, 'seq')  94.6 us
    psum x1, blocking collectives, body(): lax.psum((group_sums, group_squares), ('seq', 'head'))  43.1 us
    psum x1, blocking collectives, body(): lax.psum((jnp.sum(context, axis=0), jnp.sum(context * context, axis=0)),...  33 us
    all_gather x1, waiting for transfers between devices, body(): lax.all_gather(w_qkv, 'seq', axis=0, tiled=True)  23.2 us
    unnamed x56, local copies, waits for them, and re-layouts  14.5 us
    reduce_scatter x1, waiting for transfers between devices, body(): lax.psum_scatter(jnp.dot(attended, w_out, preferred_element_type=jnp.floa...  13.2 us
    dot_general x1, matrix products, body(): jnp.einsum('nd,dkj->nkj', modulated, lax.all_gather(w_qkv, 'seq', axis=0,...  9.7 us
    gather x1, local copies, waits for them, and re-layouts, body(): context = jnp.take(text_table, text_ids, axis=1).astype(jnp.float32)  6.18 us
  transfers between devices with their start and end apart: 7, of which 3 were waited for; matrix products, arithmetic and copies ran while one was open for 10% of the time, Pallas kernels for 0%

commit v1 on v0

--- a/solution.py
+++ b/solution.py
@@ -7,6 +7,22 @@
 HD = 128
 GN_GROUPS = 32
 eps_norm = 1e-06
+
+
+def summed_both_ways(array, axis, dim, contribution):
+    peers, index, extent = (lax.axis_size(axis), lax.axis_index(axis), array.shape[dim])
+    upward = [(i, (i + 1) % peers) for i in range(peers)]
+    left = [(i, (i - 1) % peers) for i in range(peers)]
+    half = peers // 2
+    from_left = from_right = array
+    total = contribution(array, index * extent)
+    for step in range(1, half + 1):
+        from_left = lax.ppermute(from_left, axis, upward)
+        if step < peers - half:
+            from_right = lax.ppermute(from_right, axis, left)
+            total = total + contribution(from_right, (index + step) % peers * extent)
+        total = total + contribution(from_left, (index - step) % peers * extent)
+    return total
 
 
 def with_halo(cells, sides, width):
@@ -144,11 +160,16 @@
     token_count = modulated.shape[0]
     head_width = w_qkv.shape[2]
     heads_here = head_width // HD
-    qkv = jnp.einsum(
-        "nd,dkj->nkj",
-        modulated,
-        lax.all_gather(w_qkv, "seq", axis=0, tiled=True),
-        preferred_element_type=jnp.float32,
+    qkv = summed_both_ways(
+        w_qkv,
+        "seq",
+        0,
+        lambda shard, start: jnp.einsum(
+            "nd,dkj->nkj",
+            lax.dynamic_slice_in_dim(modulated, start, shard.shape[0], axis=1),
+            shard,
+            preferred_element_type=jnp.float32,
+        ),
     ).astype(jnp.bfloat16)
     context = jnp.take(text_table, text_ids, axis=1).astype(jnp.float32)
     text_weight = w_text.astype(jnp.float32)

time: 286 us -> 455 us (1.59)
  starting transfers between devices: 6.94 us -> 134 us
  blocking collectives: 177 us -> 201 us
  waiting for transfers between devices: 38.6 us -> 45.2 us
  other arithmetic: 6.94 us -> 12.4 us
    ppermute x0 -> x15, starting transfers between devices: none -> 126 us  [the longest x8 118 us: summed_both_ways(): from_left = lax.ppermute(from_left, axis, upward)]
    ppermute x0 -> x15, waiting for transfers between devices: none -> 27.4 us  [the longest x8 27.4 us: summed_both_ways(): from_left = lax.ppermute(from_left, axis, upward)]
    all_gather x1 -> x0, waiting for transfers between devices: 23.2 us -> none  [body(): lax.all_gather(w_qkv, 'seq', axis=0, tiled=True)]
    psum x1, blocking collectives: 43.1 us -> 57.6 us  [body(): lax.psum((group_sums, group_squares), ('seq', 'head'))]
    psum x1, blocking collectives: 33 us -> 42.6 us  [body(): lax.psum((jnp.sum(context, axis=0), jnp.sum(context * context, axis=0)),...]
    dot_general x1 -> x16, matrix products: 9.7 us -> 12.7 us  [body(): jnp.einsum('nd,dkj->nkj', lax.dynamic_slice_in_dim(modulated, start, shar...]
    unnamed x56 -> x80, local copies, waits for them, and re-layouts: 14.5 us -> 15.4 us
  transfers between devices with their start and end apart: 7 -> 21, of which waited for: 3 -> 7; matrix products, arithmetic and copies ran while one was open for 10% -> 11% of each run, Pallas kernels for 0% -> 0%
where the time goes in v1:
time: 455 us; the launch traced here: 454 us
  blocking collectives  201 us (44%)
  starting transfers between devices  134 us (29%)
  waiting for transfers between devices  45.2 us (10%)
  local copies, waits for them, and re-layouts  23.6 us (5%)
  matrix products  22.3 us (5%)
  between operations  14.8 us (3%)
  other arithmetic  12.4 us (3%)
    ppermute x8, starting transfers between devices, summed_both_ways(): from_left = lax.ppermute(from_left, axis, upward)  118 us
    psum x1, blocking collectives, body(): text_kv = lax.psum(partial_kv, 'seq')  94.8 us
    psum x1, blocking collectives, body(): lax.psum((group_sums, group_squares), ('seq', 'head'))  57.6 us
    psum x1, blocking collectives, body(): lax.psum((jnp.sum(context, axis=0), jnp.sum(context * context, axis=0)),...  42.6 us
    ppermute x8, waiting for transfers between devices, summed_both_ways(): from_left = lax.ppermute(from_left, axis, upward)  27.4 us
    reduce_scatter x1, waiting for transfers between devices, body(): lax.psum_scatter(jnp.dot(attended, w_out, preferred_element_type=jnp.floa...  16.9 us
    unnamed x80, local copies, waits for them, and re-layouts  15.4 us
    dot_general x16, matrix products, body(): jnp.einsum('nd,dkj->nkj', lax.dynamic_slice_in_dim(modulated, start, shar...  12.7 us
  transfers between devices with their start and end apart: 21, of which 7 were waited for; matrix products, arithmetic and copies ran while one was open for 11% of the time, Pallas kernels for 0%

profile of v1, /device:TPU:0, one launch (start us, length us, event | category | flops | bytes accessed | tf_op | source)
XLA Modules:
  0.0 453.8 jit_solution(500498705741974509)
XLA Ops:
  6.5 5.4 %collective-permute-start.4 = (bf16[192,3,1024]{2,0,1:T(8,128)(2,1)}, bf16[192,3,1024]{2,0,1:T(8,128)(2,1)S(1)}, u32[]{:S(2)}, u32[]{:S(2)}) collective-permute-start(bf16[192,3,1024]{2,0,1:T(8,128)(2,1)} %param.24), channel_id=1, source_target_pairs={{0,30},{2,0},{4,2},{6,4},{8,6},{10,8},{12,10},{14,12},{16,14},{18,... | collective-permute-start | bytes 3538952 | tf_op jit(solution)/shard_map/ppermute | solution.py:22
  13.3 57.6 %all-reduce = (f32[32]{0:T(128)S(1)}, f32[32]{0:T(128)S(1)}) all-reduce(f32[32]{0:T(128)S(1)} %reduce_sum.92, f32[32]{0:T(128)S(1)} %reduce_sum.89), channel_id=1, replica_groups=mesh['seq'=16,'head'=2] {'seq','head'}, use_global_device_ids=true, to_apply=%region_5.6 | all-reduce | flops 64 | bytes 512 | tf_op jit(solution)/shard_map/psum | solution.py:124
  79.8 3.9 collective-permute-start.2
  85.6 10.1 %copy.82 = bf16[192,16384]{0,1:T(8,128)(2,1)} copy(bf16[192,16384]{1,0:T(8,128)(2,1)} %param.27) | data formatting | bytes 12582912 | tf_op args[11]
  95.7 6.2 %gather_fusion = bf16[512,192]{1,0:T(8,128)(2,1)S(1)} fusion(bf16[192,16384]{0,1:T(8,128)(2,1)} %copy.82, s32[1024]{0:T(1024)} %pad_clamp_fusion), kind=kCustom, calls=%fused_computation | custom fusion | bytes 395264 | tf_op jit(solution)/shard_map/jit(_take)/gather | solution.py:174
  104.9 1.7 collective-permute-start.7
  106.7 2.8 collective-permute-start.6
  109.5 13.9 %collective-permute-done.7 = bf16[192,3,1024]{2,0,1:T(8,128)(2,1)S(1)} collective-permute-done((bf16[192,3,1024]{2,0,1:T(8,128)(2,1)S(1)}, bf16[192,3,1024]{2,0,1:T(8,128)(2,1)S(1)}, u32[]{:S(2)}, u32[]{:S(2)}) %collective-permute-start.7) | collective-permute-done | bytes 1179680 | tf_op jit(solution)/shard_map/ppermute | solution.py:20
  123.4 11.1 %collective-permute-start.9 = (bf16[192,3,1024]{2,0,1:T(8,128)(2,1)S(1)}, bf16[192,3,1024]{2,0,1:T(8,128)(2,1)}, u32[]{:S(2)}, u32[]{:S(2)}) collective-permute-start(bf16[192,3,1024]{2,0,1:T(8,128)(2,1)S(1)} %collective-permute-done.7), channel_id=1, source_target_pairs={{0,2},{2,4},{4,6},{6,8},{8,10},{10,12},{12,14},{14,16},{16,18},{18... | collective-permute-start | bytes 3538952 | tf_op jit(solution)/shard_map/ppermute | solution.py:20
  135.5 6.4 %collective-permute-done.9 = bf16[192,3,1024]{2,0,1:T(8,128)(2,1)} collective-permute-done((bf16[192,3,1024]{2,0,1:T(8,128)(2,1)S(1)}, bf16[192,3,1024]{2,0,1:T(8,128)(2,1)}, u32[]{:S(2)}, u32[]{:S(2)}) %collective-permute-start.9) | collective-permute-done | bytes 1179680 | tf_op jit(solution)/shard_map/ppermute | solution.py:20
  141.9 19.7 %collective-permute-start.11 = (bf16[192,3,1024]{2,0,1:T(8,128)(2,1)}, bf16[192,3,1024]{2,0,1:T(8,128)(2,1)}, u32[]{:S(2)}, u32[]{:S(2)}) collective-permute-start(bf16[192,3,1024]{2,0,1:T(8,128)(2,1)} %collective-permute-done.9), channel_id=1, source_target_pairs={{0,2},{2,4},{4,6},{6,8},{8,10},{10,12},{12,14},{14,16},{16,18},{18... | collective-permute-start | bytes 3538952 | tf_op jit(solution)/shard_map/ppermute | solution.py:20
  164.9 23.7 %collective-permute-start.13 = (bf16[192,3,1024]{2,0,1:T(8,128)(2,1)}, bf16[192,3,1024]{2,0,1:T(8,128)(2,1)S(1)}, u32[]{:S(2)}, u32[]{:S(2)}) collective-permute-start(bf16[192,3,1024]{2,0,1:T(8,128)(2,1)} %collective-permute-done.11), channel_id=1, source_target_pairs={{0,2},{2,4},{4,6},{6,8},{8,10},{10,12},{12,14},{14,16},{16,18},{18... | collective-permute-start | bytes 3538952 | tf_op jit(solution)/shard_map/ppermute | solution.py:20
  189.0 6.5 %all_gather.6 = bf16[32,3072]{1,0:T(8,128)(2,1)S(1)} all-gather(bf16[16,3072]{1,0:T(8,128)(2,1)S(1)} %add_convert_fusion.1), channel_id=1, replica_groups=mesh['seq'=16,'head'=2] {'head'}, dimensions={0}, use_global_device_ids=true | all-gather | bytes 294912 | tf_op jit(solution)/shard_map/all_gather | solution.py:159
  195.5 21.0 %collective-permute-start.15 = (bf16[192,3,1024]{2,0,1:T(8,128)(2,1)S(1)}, bf16[192,3,1024]{2,0,1:T(8,128)(2,1)S(1)}, u32[]{:S(2)}, u32[]{:S(2)}) collective-permute-start(bf16[192,3,1024]{2,0,1:T(8,128)(2,1)S(1)} %collective-permute-done.13), channel_id=1, source_target_pairs={{0,2},{2,4},{4,6},{6,8},{8,10},{10,12},{12,14},{14,16},{16,18},{18... | collective-permute-start | bytes 3538952 | tf_op jit(solution)/shard_map/ppermute | solution.py:20
  216.9 1.8 convolution_add_fusion.9
  220.4 5.2 %collective-permute-done.15 = bf16[192,3,1024]{2,0,1:T(8,128)(2,1)S(1)} collective-permute-done((bf16[192,3,1024]{2,0,1:T(8,128)(2,1)S(1)}, bf16[192,3,1024]{2,0,1:T(8,128)(2,1)S(1)}, u32[]{:S(2)}, u32[]{:S(2)}) %collective-permute-start.15) | collective-permute-done | bytes 1179680 | tf_op jit(solution)/shard_map/ppermute | solution.py:20
  225.6 19.1 %collective-permute-start.17 = (bf16[192,3,1024]{2,0,1:T(8,128)(2,1)S(1)}, bf16[192,3,1024]{2,0,1:T(8,128)(2,1)S(1)}, u32[]{:S(2)}, u32[]{:S(2)}) collective-permute-start(bf16[192,3,1024]{2,0,1:T(8,128)(2,1)S(1)} %collective-permute-done.15), channel_id=1, source_target_pairs={{0,2},{2,4},{4,6},{6,8},{8,10},{10,12},{12,14},{14,16},{16,18},{18... | collective-permute-start | bytes 3538952 | tf_op jit(solution)/shard_map/ppermute | solution.py:20
  251.8 21.2 %collective-permute-start.18 = (bf16[192,3,1024]{2,0,1:T(8,128)(2,1)S(1)}, bf16[192,3,1024]{2,0,1:T(8,128)(2,1)S(1)}, u32[]{:S(2)}, u32[]{:S(2)}) collective-permute-start(bf16[192,3,1024]{2,0,1:T(8,128)(2,1)S(1)} %collective-permute-done.17), channel_id=1, source_target_pairs={{0,2},{2,4},{4,6},{6,8},{8,10},{10,12},{12,14},{14,16},{16,18},{18... | collective-permute-start | bytes 3538952 | tf_op jit(solution)/shard_map/ppermute | solution.py:20
  278.0 42.6 %all-reduce.1 = (f32[512]{0:T(512)S(1)}, f32[512]{0:T(512)S(1)}) all-reduce(f32[512]{0:T(512)S(1)} %get-tuple-element.16, f32[512]{0:T(512)S(1)} %get-tuple-element.15), channel_id=1, replica_groups=mesh['seq'=16,'head'=2] {'seq'}, use_global_device_ids=true, to_apply=%region_9.10 | all-reduce | flops 1024 | bytes 8192 | tf_op jit(solution)/shard_map/psum | solution.py:178
  320.6 3.9 fusion.19
  324.5 94.8 %all-reduce.3 = bf16[512,2,1024]{2,0,1:T(8,128)(2,1)S(1)} all-reduce(f32[512,2,1024]{2,0,1:T(8,128)} %fusion.19), channel_id=1, replica_groups=mesh['seq'=16,'head'=2] {'seq'}, use_global_device_ids=true, to_apply=%region_10.11 | all-reduce | flops 1048576 | bytes 6291456 | tf_op jit(solution)/shard_map/psum | solution.py:187
  422.2 2.4 copy.103
  426.5 2.0 fusion.49
  428.5 16.9 %reduce-scatter.2.cloned.1.call-done = f32[16,3072]{1,0:T(8,128)} async-done(((f32[32,3072]{1,0:T(8,128)}), f32[16,3072]{1,0:T(8,128)}) %reduce-scatter.2.cloned.1.call-update) | async-done | bytes 196624 | tf_op jit(solution)/shard_map/reduce_scatter | solution.py:203
  (172 shorter events, 39.3 us)
Async XLA Ops:
  6.5 314.1 %copy-start = (bf16[192,2,1024]{2,1,0:T(2,128)(2,1)S(1)}, bf16[192,2,1024]{2,1,0:T(2,128)(2,1)}, u32[]{:S(2)}) copy-start(bf16[192,2,1024]{2,1,0:T(2,128)(2,1)} %param.29) | copy-start | bytes 2359300
  6.5 415.6 %all-gather.2.cloned.1.call-start = ((), (), s32[]{:S(2)}) async-start(), calls=%async_computation.1 | async-start | bytes 2228224 | tf_op jit(solution)/shard_map/all_gather | solution.py:197
  6.5 100.1 %collective-permute-start.4 = (bf16[192,3,1024]{2,0,1:T(8,128)(2,1)}, bf16[192,3,1024]{2,0,1:T(8,128)(2,1)S(1)}, u32[]{:S(2)}, u32[]{:S(2)}) collective-permute-start(bf16[192,3,1024]{2,0,1:T(8,128)(2,1)} %param.24), channel_id=1, source_target_pairs={{0,30},{2,0},{4,2},{6,4},{8,6},{10,8},{12,10},{14,12},{16,14},{18,... | collective-permute-start | bytes 3538952 | tf_op jit(solution)/shard_map/ppermute | solution.py:22
  13.2 91.6 %collective-permute-start.5 = (bf16[192,3,1024]{2,0,1:T(8,128)(2,1)}, bf16[192,3,1024]{2,0,1:T(8,128)(2,1)S(1)}, u32[]{:S(2)}, u32[]{:S(2)}) collective-permute-start(bf16[192,3,1024]{2,0,1:T(8,128)(2,1)} %param.24), channel_id=1, source_target_pairs={{0,2},{2,4},{4,6},{6,8},{8,10},{10,12},{12,14},{14,16},{16,18},{18... | collective-permute-start | bytes 3538952 | tf_op jit(solution)/shard_map/ppermute | solution.py:20
  72.2 6.1 %collective-permute-start = (bf16[8,1,4,512]{3,0,2,1:T(8,128)(2,1)S(1)}, bf16[8,1,4,512]{3,0,2,1:T(8,128)(2,1)S(1)}, u32[]{:S(2)}, u32[]{:S(2)}) collective-permute-start(bf16[8,1,4,512]{3,0,2,1:T(8,128)(2,1)S(1)} %get-tuple-element.41), channel_id=1, source_target_pairs={{0,2},{2,4},{4,6},{6,8},{8,10},{10,12},{12,14},{14,16},{16,18},{18... | collective-permute-start | bytes 98312 | tf_op jit(solution)/shard_map/ppermute | solution.py:36
  73.5 5.6 %collective-permute-start.1 = (bf16[8,1,4,512]{3,0,2,1:T(8,128)(2,1)S(1)}, bf16[8,1,4,512]{3,0,2,1:T(8,128)(2,1)S(1)}, u32[]{:S(2)}, u32[]{:S(2)}) collective-permute-start(bf16[8,1,4,512]{3,0,2,1:T(8,128)(2,1)S(1)} %get-tuple-element.42), channel_id=1, source_target_pairs={{2,0},{4,2},{6,4},{8,6},{10,8},{12,10},{14,12},{16,14},{18,16},{20... | collective-permute-start | bytes 98312 | tf_op jit(solution)/shard_map/ppermute | solution.py:38
  79.8 22.1 %collective-permute-start.2 = (bf16[8,4,1,512]{3,0,2,1:T(8,128)(2,1)}, bf16[8,4,1,512]{3,0,2,1:T(8,128)(2,1)}, u32[]{:S(2)}, u32[]{:S(2)}) collective-permute-start(bf16[8,4,1,512]{3,0,2,1:T(8,128)(2,1)} %get-tuple-element.39), channel_id=1, source_target_pairs={{0,1},{2,3},{4,5},{6,7},{8,9},{10,11},{12,13},{14,15},{16,17},{18,... | collective-permute-start | bytes 98312 | tf_op jit(solution)/shard_map/ppermute | solution.py:36
  83.7 18.2 %collective-permute-start.3 = (bf16[8,4,1,512]{3,0,2,1:T(8,128)(2,1)}, bf16[8,4,1,512]{3,0,2,1:T(8,128)(2,1)}, u32[]{:S(2)}, u32[]{:S(2)}) collective-permute-start(bf16[8,4,1,512]{3,0,2,1:T(8,128)(2,1)} %get-tuple-element.40), channel_id=1, source_target_pairs={{1,0},{3,2},{5,4},{7,6},{9,8},{11,10},{13,12},{15,14},{17,16},{19,... | collective-permute-start | bytes 98312 | tf_op jit(solution)/shard_map/ppermute | solution.py:38
  103.8 57.9 %copy-start.12 = (bf16[3,3,3,16,512]{4,3,2,1,0:T(8,128)(2,1)S(1)}, bf16[3,3,3,16,512]{4,3,2,1,0:T(8,128)(2,1)}, u32[]{:S(2)}) copy-start(bf16[3,3,3,16,512]{4,3,2,1,0:T(8,128)(2,1)} %param.19) | copy-start | bytes 1327108
  103.9 57.9 %copy-start.21 = (f32[16]{0:T(128)S(1)}, f32[16]{0:T(128)}, u32[]{:S(2)}) copy-start(f32[16]{0:T(128)} %param.20) | copy-start | bytes 196
  104.9 18.5 %collective-permute-start.7 = (bf16[192,3,1024]{2,0,1:T(8,128)(2,1)S(1)}, bf16[192,3,1024]{2,0,1:T(8,128)(2,1)S(1)}, u32[]{:S(2)}, u32[]{:S(2)}) collective-permute-start(bf16[192,3,1024]{2,0,1:T(8,128)(2,1)S(1)} %collective-permute-done.5), channel_id=1, source_target_pairs={{0,2},{2,4},{4,6},{6,8},{8,10},{10,12},{12,14},{14,16},{16,18},{18... | collective-permute-start | bytes 3538952 | tf_op jit(solution)/shard_map/ppermute | solution.py:20
  106.7 28.6 %collective-permute-start.6 = (bf16[192,3,1024]{2,0,1:T(8,128)(2,1)S(1)}, bf16[192,3,1024]{2,0,1:T(8,128)(2,1)S(1)}, u32[]{:S(2)}, u32[]{:S(2)}) collective-permute-start(bf16[192,3,1024]{2,0,1:T(8,128)(2,1)S(1)} %collective-permute-done.4), channel_id=1, source_target_pairs={{0,30},{2,0},{4,2},{6,4},{8,6},{10,8},{12,10},{14,12},{16,14},{18,... | collective-permute-start | bytes 3538952 | tf_op jit(solution)/shard_map/ppermute | solution.py:22
  123.4 18.5 %collective-permute-start.9 = (bf16[192,3,1024]{2,0,1:T(8,128)(2,1)S(1)}, bf16[192,3,1024]{2,0,1:T(8,128)(2,1)}, u32[]{:S(2)}, u32[]{:S(2)}) collective-permute-start(bf16[192,3,1024]{2,0,1:T(8,128)(2,1)S(1)} %collective-permute-done.7), channel_id=1, source_target_pairs={{0,2},{2,4},{4,6},{6,8},{8,10},{10,12},{12,14},{14,16},{16,18},{18... | collective-permute-start | bytes 3538952 | tf_op jit(solution)/shard_map/ppermute | solution.py:20
  135.3 26.4 %collective-permute-start.8 = (bf16[192,3,1024]{2,0,1:T(8,128)(2,1)S(1)}, bf16[192,3,1024]{2,0,1:T(8,128)(2,1)}, u32[]{:S(2)}, u32[]{:S(2)}) collective-permute-start(bf16[192,3,1024]{2,0,1:T(8,128)(2,1)S(1)} %collective-permute-done.6), channel_id=1, source_target_pairs={{0,30},{2,0},{4,2},{6,4},{8,6},{10,8},{12,10},{14,12},{16,14},{18,... | collective-permute-start | bytes 3538952 | tf_op jit(solution)/shard_map/ppermute | solution.py:22
  141.9 23.0 %collective-permute-start.11 = (bf16[192,3,1024]{2,0,1:T(8,128)(2,1)}, bf16[192,3,1024]{2,0,1:T(8,128)(2,1)}, u32[]{:S(2)}, u32[]{:S(2)}) collective-permute-start(bf16[192,3,1024]{2,0,1:T(8,128)(2,1)} %collective-permute-done.9), channel_id=1, source_target_pairs={{0,2},{2,4},{4,6},{6,8},{8,10},{10,12},{12,14},{14,16},{16,18},{18... | collective-permute-start | bytes 3538952 | tf_op jit(solution)/shard_map/ppermute | solution.py:20
  161.7 27.2 %collective-permute-start.10 = (bf16[192,3,1024]{2,0,1:T(8,128)(2,1)}, bf16[192,3,1024]{2,0,1:T(8,128)(2,1)}, u32[]{:S(2)}, u32[]{:S(2)}) collective-permute-start(bf16[192,3,1024]{2,0,1:T(8,128)(2,1)} %collective-permute-done.8), channel_id=1, source_target_pairs={{0,30},{2,0},{4,2},{6,4},{8,6},{10,8},{12,10},{14,12},{16,14},{18,... | collective-permute-start | bytes 3538952 | tf_op jit(solution)/shard_map/ppermute | solution.py:22
  164.9 30.6 %collective-permute-start.13 = (bf16[192,3,1024]{2,0,1:T(8,128)(2,1)}, bf16[192,3,1024]{2,0,1:T(8,128)(2,1)S(1)}, u32[]{:S(2)}, u32[]{:S(2)}) collective-permute-start(bf16[192,3,1024]{2,0,1:T(8,128)(2,1)} %collective-permute-done.11), channel_id=1, source_target_pairs={{0,2},{2,4},{4,6},{6,8},{8,10},{10,12},{12,14},{14,16},{16,18},{18... | collective-permute-start | bytes 3538952 | tf_op jit(solution)/shard_map/ppermute | solution.py:20
  188.8 30.7 %collective-permute-start.12 = (bf16[192,3,1024]{2,0,1:T(8,128)(2,1)}, bf16[192,3,1024]{2,0,1:T(8,128)(2,1)S(1)}, u32[]{:S(2)}, u32[]{:S(2)}) collective-permute-start(bf16[192,3,1024]{2,0,1:T(8,128)(2,1)} %collective-permute-done.10), channel_id=1, source_target_pairs={{0,30},{2,0},{4,2},{6,4},{8,6},{10,8},{12,10},{14,12},{16,14},{18,... | collective-permute-start | bytes 3538952 | tf_op jit(solution)/shard_map/ppermute | solution.py:22
  195.5 30.1 %collective-permute-start.15 = (bf16[192,3,1024]{2,0,1:T(8,128)(2,1)S(1)}, bf16[192,3,1024]{2,0,1:T(8,128)(2,1)S(1)}, u32[]{:S(2)}, u32[]{:S(2)}) collective-permute-start(bf16[192,3,1024]{2,0,1:T(8,128)(2,1)S(1)} %collective-permute-done.13), channel_id=1, source_target_pairs={{0,2},{2,4},{4,6},{6,8},{8,10},{10,12},{12,14},{14,16},{16,18},{18... | collective-permute-start | bytes 3538952 | tf_op jit(solution)/shard_map/ppermute | solution.py:20
  219.5 31.9 %collective-permute-start.14 = (bf16[192,3,1024]{2,0,1:T(8,128)(2,1)S(1)}, bf16[192,3,1024]{2,0,1:T(8,128)(2,1)S(1)}, u32[]{:S(2)}, u32[]{:S(2)}) collective-permute-start(bf16[192,3,1024]{2,0,1:T(8,128)(2,1)S(1)} %collective-permute-done.12), channel_id=1, source_target_pairs={{0,30},{2,0},{4,2},{6,4},{8,6},{10,8},{12,10},{14,12},{16,14},{18,... | collective-permute-start | bytes 3538952 | tf_op jit(solution)/shard_map/ppermute | solution.py:22
  225.6 26.2 %collective-permute-start.17 = (bf16[192,3,1024]{2,0,1:T(8,128)(2,1)S(1)}, bf16[192,3,1024]{2,0,1:T(8,128)(2,1)S(1)}, u32[]{:S(2)}, u32[]{:S(2)}) collective-permute-start(bf16[192,3,1024]{2,0,1:T(8,128)(2,1)S(1)} %collective-permute-done.15), channel_id=1, source_target_pairs={{0,2},{2,4},{4,6},{6,8},{8,10},{10,12},{12,14},{14,16},{16,18},{18... | collective-permute-start | bytes 3538952 | tf_op jit(solution)/shard_map/ppermute | solution.py:20
  251.4 23.2 %collective-permute-start.16 = (bf16[192,3,1024]{2,0,1:T(8,128)(2,1)S(1)}, bf16[192,3,1024]{2,0,1:T(8,128)(2,1)S(1)}, u32[]{:S(2)}, u32[]{:S(2)}) collective-permute-start(bf16[192,3,1024]{2,0,1:T(8,128)(2,1)S(1)} %collective-permute-done.14), channel_id=1, source_target_pairs={{0,30},{2,0},{4,2},{6,4},{8,6},{10,8},{12,10},{14,12},{16,14},{18,... | collective-permute-start | bytes 3538952 | tf_op jit(solution)/shard_map/ppermute | solution.py:22
  251.8 24.0 %collective-permute-start.18 = (bf16[192,3,1024]{2,0,1:T(8,128)(2,1)S(1)}, bf16[192,3,1024]{2,0,1:T(8,128)(2,1)S(1)}, u32[]{:S(2)}, u32[]{:S(2)}) collective-permute-start(bf16[192,3,1024]{2,0,1:T(8,128)(2,1)S(1)} %collective-permute-done.17), channel_id=1, source_target_pairs={{0,2},{2,4},{4,6},{6,8},{8,10},{10,12},{12,14},{14,16},{16,18},{18... | collective-permute-start | bytes 3538952 | tf_op jit(solution)/shard_map/ppermute | solution.py:20
  277.6 167.8 %reduce-scatter.2.cloned.1.call-start = ((), (), s32[]{:S(2)}) async-start(), calls=%async_computation.2 | async-start | bytes 589824 | tf_op jit(solution)/shard_map/reduce_scatter | solution.py:203
  (22 other events, 528.3 us)
Sparse Core Ops, SparseCore 0:
  277.7 59.3 all-gather.1
  428.6 16.6 reduce-scatter.1
